TPU v7x, 256 devices: a whole 4x4x8 slice. The times are simulated.
256 devices in a mesh: lat: 64 (over x, y_lo, z), coh: 4 (over y_hi, core).
Axes of the slice: x: 4, y: 4 (y_hi: 2, y_lo: 2; y = y_hi * 2 + y_lo), z: 8, core: 2. Of those that a mesh axis runs over, the one named last changes fastest.
Arguments:
- density: float32 [128, 2, 512, 1024], P('coh', None, 'lat'), may hold values from 0.1 to 1
- cotangent: float32 [128, 2, 512, 1024], P('coh', None, 'lat'), may hold values from -0.5 to 1.5
- land_mask: int32 [2, 512, 1024], P(None, 'lat'), may hold values 0 or 1
- east_vel: float32 [2, 512, 1024], P(None, 'lat'), may hold values from -0.4 to 0.4
- north_vel: float32 [2, 512, 1024], P(None, 'lat'), may hold values from -0.4 to 0.4
- diffusion: float32 [2, 512, 1024], P(None, 'lat'), may hold values from 0.02 to 0.2
- age_class: int32 [128], P('coh'), may hold values from 0 to 31, as said below
- mort_rate: float32 [32], replicated, may hold values from 0.05 to 0.5
- crowd_coef: float32 [32], replicated, may hold values from 1 to 4
- mass: float32 [32], replicated, may hold values from 0.5 to 2
- speed: float32 [32], replicated, may hold values from 0.25 to 1
Outputs:
- grad_density: float32 [128, 2, 512, 1024], P('coh', None, 'lat')
- grad_east_vel: float32 [2, 512, 1024], P(None, 'lat', 'coh')
- grad_north_vel: float32 [2, 512, 1024], P(None, 'lat', 'coh')
- grad_diffusion: float32 [2, 512, 1024], P(None, 'lat', 'coh')
Inputs may be any that keep to these rules, and one draw needn't show every extreme that they name: `age_class`: each age class is held by exactly 4 cohorts.
All inputs are finite; a program needn't handle non-finite values. No bound on the sum of `land_mask` on one device may be relied on, other than what follows from the above.
Results may differ from a plain program's by a relative error of at most 0.00014.
Values sent between devices are 32-bit elements; how exact they have to be, the bound alone decides.
No kernel may reach another device: no remote copies, remote signals or barrier semaphores. Data moves between devices by JAX's collectives and lax.ppermute only.
A program may use at most 128 MiB of HBM per device.

v0:
```python
import jax
import jax.numpy as jnp
from jax import lax
from jax.sharding import PartitionSpec as P

COH = 128
STEPS = 2


def extended(value, sides, width):
    for axis, dim in sides:
        devices, length = (lax.axis_size(axis), value.shape[dim])
        up = [(i, (i + 1) % devices) for i in range(devices - 1)]
        down = [(j, i) for i, j in up]
        last = lax.slice_in_dim(value, length - width, length, axis=dim)
        first = lax.slice_in_dim(value, 0, width, axis=dim)
        before = lax.ppermute(last, axis, up)
        after = lax.ppermute(first, axis, down)
        value = jnp.concatenate([before, value, after], axis=dim)
    return value


def lookup(age_class, mort_rate, crowd_coef, mass, speed):
    classes = jnp.arange(mort_rate.shape[0], dtype=jnp.int32)
    onehot = (age_class[:, None] == classes[None, :]).astype(jnp.float32)
    tables = jnp.stack([mort_rate, crowd_coef, mass, speed], axis=1)
    picked = jnp.dot(onehot, tables, precision=lax.Precision.HIGHEST)
    return [picked[:, column][:, None, None, None] for column in range(4)]


def local(
    density,
    cotangent,
    land_mask,
    east_vel,
    north_vel,
    diffusion,
    age_class,
    mort_rate,
    crowd_coef,
    mass,
    speed,
):
    ocean = land_mask.astype(jnp.float32)[None]
    mortal, crowding, weight, swim = lookup(age_class, mort_rate, crowd_coef, mass, speed)
    east_coef = swim * east_vel[None]
    north_coef = swim * north_vel[None]
    kappa = diffusion[None]
    state = density
    saved = []
    for section in range(STEPS):
        crowd = lax.psum(jnp.sum(weight * state, axis=0), "coh") / COH
        survival = jnp.exp(-(mortal + crowding * crowd[None]))
        survived = state * survival
        wet = ocean * survived
        padded = extended(wet, (("lat", 2),), 1)
        north_val = padded[:, :, 2:]
        south_val = padded[:, :, :-2]
        east_val = jnp.roll(wet, -1, axis=3)
        west_val = jnp.roll(wet, 1, axis=3)
        laplace = north_val + south_val + east_val + west_val - 4.0 * wet
        east_diff = 0.5 * (east_val - west_val)
        north_diff = 0.5 * (north_val - south_val)
        state = ocean * (wet + kappa * laplace - east_coef * east_diff - north_coef * north_diff)
        saved.append((survival, survived, laplace, east_diff, north_diff))
    adjoint = cotangent
    shares = None
    for section in reversed(range(STEPS)):
        survival, survived, laplace, east_diff, north_diff = saved[section]
        masked = ocean * adjoint
        grad_east = -jnp.sum(masked * swim * east_diff, axis=0)
        grad_north = -jnp.sum(masked * swim * north_diff, axis=0)
        grad_kappa = jnp.sum(masked * laplace, axis=0)
        pieces = (
            lax.psum_scatter(grad_east, "coh", scatter_dimension=2, tiled=True),
            lax.psum_scatter(grad_north, "coh", scatter_dimension=2, tiled=True),
            lax.psum_scatter(grad_kappa, "coh", scatter_dimension=2, tiled=True),
        )
        shares = pieces if shares is None else jax.tree.map(jnp.add, shares, pieces)
        to_north = (kappa - 0.5 * north_coef) * masked
        to_south = (kappa + 0.5 * north_coef) * masked
        to_east = (kappa - 0.5 * east_coef) * masked
        to_west = (kappa + 0.5 * east_coef) * masked
        stacked = extended(jnp.stack([to_north, to_south]), (("lat", 3),), 1)
        from_below = stacked[0][:, :, :-2]
        from_above = stacked[1][:, :, 2:]
        grad_wet = (
            (1.0 - 4.0 * kappa) * masked
            + jnp.roll(to_east, 1, axis=3)
            + jnp.roll(to_west, -1, axis=3)
            + from_below
            + from_above
        )
        grad_surv = ocean * grad_wet
        pressure = lax.psum(jnp.sum(-crowding * grad_surv * survived, axis=0), "coh")
        adjoint = grad_surv * survival + weight / COH * pressure[None]
    return (adjoint, shares[0], shares[1], shares[2])


def solution(mesh):
    in_specs = (
        P("coh", None, "lat", None),
        P("coh", None, "lat", None),
        P(None, "lat", None),
        P(None, "lat", None),
        P(None, "lat", None),
        P(None, "lat", None),
        P("coh"),
        P(),
        P(),
        P(),
        P(),
    )
    out_specs = (
        P("coh", None, "lat", None),
        P(None, "lat", "coh"),
        P(None, "lat", "coh"),
        P(None, "lat", "coh"),
    )
    return jax.shard_map(local, mesh=mesh, in_specs=in_specs, out_specs=out_specs, check_vma=False)
```

profile of v0, /device:TPU:1, one launch (start us, length us, event | category | flops | bytes accessed | tf_op | source)
XLA Modules:
  0.0 388.2 jit_solution(14787665174152883794)
XLA Ops:
  8.1 3.5 multiply_reduce_fusion.9
  11.7 49.5 %all-reduce.5.cloned.1.call-done = f32[2,8,1024]{2,1,0:T(8,128)} async-done(((f32[2,8,1024]{2,1,0:T(8,128)}), f32[2,8,1024]{2,1,0:T(8,128)}) %all-reduce.5.cloned.1.call-update) | async-done | bytes 65552 | tf_op jit(solution)/shard_map/psum | solution.py:52
  62.0 3.0 fusion.26
  65.0 3.2 collective-permute-start.3
  70.6 3.1 collective-permute-done.3
  73.8 4.0 %collective-permute-done.2 = f32[32,2,1,1024]{3,0,2,1:T(8,128)S(1)} collective-permute-done((f32[32,2,1,1024]{3,0,2,1:T(8,128)S(1)}, f32[32,2,1,1024]{3,0,2,1:T(8,128)S(1)}, u32[]{:S(2)}, u32[]{:S(2)}) %collective-permute-start.2) | collective-permute-done | bytes 262176 | tf_op jit(solution)/shard_map/ppermute | solution.py:18
  77.8 5.9 %fusion.9 = (f32[32,2,8,1024]{3,0,2,1:T(8,128)}, f32[32,2,8,1024]{3,0,2,1:T(8,128)}, f32[1,32,2,8,1024]{4,1,3,2,0:T(8,128)S(1)}, f32[1,32,2,8,1024]{4,1,3,2,0:T(...) fusion(f32[2,8,1024]{2,1,0:T(8,128)S(1)} %copy-done.22, f32[32]{0:T(128)S(1)} %get-tuple-element.58, ...), kind=kLoop, calls=%fused_computation.15 | loop fusion | flops 18333696 | bytes 19726592 | tf_op jit(solution)/shard_map/mul | solution.py:82
  87.4 4.8 %collective-permute-start = (f32[2,32,2,1,1024]{4,1,3,2,0:T(8,128)}, f32[2,32,2,1,1024]{4,1,3,2,0:T(8,128)}, u32[]{:S(2)}, u32[]{:S(2)}) collective-permute-start(f32[2,32,2,1,1024]{4,1,3,2,0:T(8,128)} %get-tuple-element.27), channel_id=1, source_target_pairs={{0,4},{4,8},{8,12},{12,16},{16,20},{20,24},{24,28},{28,32},{32,36}... | collective-permute-start | bytes 1572872 | tf_op jit(solution)/shard_map/ppermute | solution.py:17
  94.4 3.5 slice.170
  99.7 41.5 %all-reduce.7.cloned.1.call-done = f32[2,8,1024]{2,1,0:T(8,128)} async-done(((f32[2,8,1024]{2,1,0:T(8,128)}), f32[2,8,1024]{2,1,0:T(8,128)}) %all-reduce.7.cloned.1.call-update) | async-done | bytes 65552 | tf_op jit(solution)/shard_map/psum | solution.py:52
  142.1 3.1 pad_maximum_fusion
  148.7 4.5 %multiply_reduce_fusion.7 = (f32[2,8,1024]{2,1,0:T(8,128)}, f32[32,2,8,1024]{3,0,2,1:T(8,128)}, f32[32,2,8,1024]{3,0,2,1:T(8,128)S(1)}) fusion(f32[32,2,8,1024]{3,0,2,1:T(8,128)S(1)} %copy-done.13, f32[32]{0:T(128)S(1)} %get-tuple-element.57, f32[2,8,1024]{2,1,0:T(8,128)S(1)} %broadcast_multiply_fusion, f32[32]{0:T(128)S(1)} %get-tuple-element.60, ...), kind=kLoop, calls=%fused_computation.57 | loop fusion | flops 8896512 | bytes 17039744 | tf_op jit(solution)/shard_map/reduce_sum | solution.py:95
  153.3 2.9 fusion.42
  160.3 4.7 %collective-permute-start.7 = (f32[32,2,1,1024]{3,0,2,1:T(8,128)}, f32[32,2,1,1024]{3,0,2,1:T(8,128)}, u32[]{:S(2)}, u32[]{:S(2)}) collective-permute-start(f32[32,2,1,1024]{3,0,2,1:T(8,128)} %get-tuple-element.42), channel_id=1, source_target_pairs={{0,4},{4,8},{8,12},{12,16},{16,20},{20,24},{24,28},{28,32},{32,36}... | collective-permute-start | bytes 786440 | tf_op jit(solution)/shard_map/ppermute | solution.py:17
  165.0 36.8 %all-reduce.9.cloned.1.call-done = f32[2,8,1024]{2,1,0:T(8,128)} async-done(((f32[2,8,1024]{2,1,0:T(8,128)}), f32[2,8,1024]{2,1,0:T(8,128)}) %all-reduce.9.cloned.1.call-update) | async-done | bytes 65552 | tf_op jit(solution)/shard_map/psum | solution.py:95
  201.7 5.3 %multiply_reduce_fusion = (f32[2,8,1024]{2,1,0:T(8,128)}, f32[2,8,1024]{2,1,0:T(8,128)}, f32[2,8,1024]{2,1,0:T(8,128)}, f32[32,2,8,1024]{3,0,2,1:T(8,128)S(1)}) fusion(f32[32,2,8,1024]{3,0,2,1:T(8,128)S(1)} %fusion.26, f32[32,2,8,1023]{3,0,2,1:T(8,128)} %copy-done.6, f32[32,2,8,1]{3,0,2,1:T(8,128)S(1)} %get-tuple-element.53, ...), kind=kLoop, calls=%fused_computation.48 | loop fusion | flops 14106624 | bytes 11403776 | tf_op jit(solution)/shard_map/reduce_sum | solution.py:73
  210.5 4.2 %collective-permute-start.4 = (f32[2,32,2,1,1024]{4,1,3,2,0:T(8,128)S(1)}, f32[2,32,2,1,1024]{4,1,3,2,0:T(8,128)S(1)}, u32[]{:S(2)}, u32[]{:S(2)}) collective-permute-start(f32[2,32,2,1,1024]{4,1,3,2,0:T(8,128)S(1)} %get-tuple-element.25), channel_id=1, source_target_pairs={{0,4},{4,8},{8,12},{12,16},{16,20},{20,24},{24,28},{28,32},{32,36}... | collective-permute-start | bytes 1572872 | tf_op jit(solution)/shard_map/ppermute | solution.py:17
  214.9 4.7 %multiply_reduce_fusion.1 = (f32[2,8,1024]{2,1,0:T(8,128)}, f32[2,8,1024]{2,1,0:T(8,128)}, f32[2,8,1024]{2,1,0:T(8,128)}) fusion(f32[32,2,8,1024]{3,0,2,1:T(8,128)S(1)} %copy-done.1, f32[32,2,8,1023]{3,0,2,1:T(8,128)S(1)} %copy-done.12, f32[32,2,8,1]{3,0,2,1:T(8,128)S(1)} %copy-done.16, f32[32,2,8,1]{3,0,2,1:T(8,128)S(1)} %get-tuple-element.46, ...), kind=kLoop, calls=%fused_computation.49 | loop fusion | flops 10960896 | bytes 9175168 | tf_op jit(solution)/shard_map/reduce_sum | solution.py:73
  219.6 5.1 %collective-permute-done.5 = f32[2,32,2,1,1024]{4,1,3,2,0:T(8,128)S(1)} collective-permute-done((f32[2,32,2,1,1024]{4,1,3,2,0:T(8,128)S(1)}, f32[2,32,2,1,1024]{4,1,3,2,0:T(8,128)S(1)}, u32[]{:S(2)}, u32[]{:S(2)}) %collective-permute-start.5) | collective-permute-done | bytes 524320 | tf_op jit(solution)/shard_map/ppermute | solution.py:18
  228.1 3.6 multiply_reduce_fusion.6
  233.9 45.8 %all-reduce.11.cloned.1.call-done = f32[2,8,1024]{2,1,0:T(8,128)} async-done(((f32[2,8,1024]{2,1,0:T(8,128)}), f32[2,8,1024]{2,1,0:T(8,128)}) %all-reduce.11.cloned.1.call-update) | async-done | bytes 65552 | tf_op jit(solution)/shard_map/psum | solution.py:95
  283.7 29.2 %reduce-scatter.4.cloned.1.call-done = f32[2,8,256]{2,1,0:T(8,128)} async-done(((f32[2,8,1024]{2,1,0:T(8,128)}), f32[2,8,256]{2,1,0:T(8,128)}) %reduce-scatter.4.cloned.1.call-update) | async-done | bytes 16400 | tf_op jit(solution)/shard_map/reduce_scatter | solution.py:75
  312.9 34.2 %reduce-scatter.6.cloned.1.call-done = f32[2,8,256]{2,1,0:T(8,128)} async-done(((f32[2,8,1024]{2,1,0:T(8,128)}), f32[2,8,256]{2,1,0:T(8,128)}) %reduce-scatter.6.cloned.1.call-update) | async-done | bytes 16400 | tf_op jit(solution)/shard_map/reduce_scatter | solution.py:76
  347.0 34.3 %reduce-scatter.8.cloned.1.call-done = f32[2,8,256]{2,1,0:T(8,128)} async-done(((f32[2,8,1024]{2,1,0:T(8,128)}), f32[2,8,256]{2,1,0:T(8,128)}) %reduce-scatter.8.cloned.1.call-update) | async-done | bytes 16400 | tf_op jit(solution)/shard_map/reduce_scatter | solution.py:77
  (119 shorter events, 33.3 us)
Async XLA Ops:
  7.2 54.0 %all-reduce.5.cloned.1.call-start = ((), (), s32[]{:S(2)}) async-start(), calls=%async_computation.3 | async-start | bytes 131072 | tf_op jit(solution)/shard_map/psum | solution.py:52
  11.6 129.6 %all-reduce.7.cloned.1.call-start = ((), (), s32[]{:S(2)}) async-start(), calls=%async_computation.4 | async-start | bytes 131072 | tf_op jit(solution)/shard_map/psum | solution.py:52
  65.0 8.7 %collective-permute-start.3 = (f32[32,2,1,1024]{3,0,2,1:T(8,128)S(1)}, f32[32,2,1,1024]{3,0,2,1:T(8,128)S(1)}, u32[]{:S(2)}, u32[]{:S(2)}) collective-permute-start(f32[32,2,1,1024]{3,0,2,1:T(8,128)S(1)} %get-tuple-element.49), channel_id=1, source_target_pairs={{0,4},{4,8},{8,12},{12,16},{16,20},{20,24},{24,28},{28,32},{32,36}... | collective-permute-start | bytes 786440 | tf_op jit(solution)/shard_map/ppermute | solution.py:17
  68.2 9.5 %copy-start.17 = (f32[2,8,1024]{2,1,0:T(8,128)S(1)}, f32[2,8,1024]{2,1,0:T(8,128)}, u32[]{:S(2)}) copy-start(f32[2,8,1024]{2,1,0:T(8,128)} %param.16) | copy-start | bytes 196612
  68.3 9.5 %copy-start.22 = (f32[2,8,1024]{2,1,0:T(8,128)S(1)}, f32[2,8,1024]{2,1,0:T(8,128)}, u32[]{:S(2)}) copy-start(f32[2,8,1024]{2,1,0:T(8,128)} %param.14) | copy-start | bytes 196612
  68.3 9.5 %copy-start.24 = (f32[2,8,1024]{2,1,0:T(8,128)S(1)}, f32[2,8,1024]{2,1,0:T(8,128)}, u32[]{:S(2)}) copy-start(f32[2,8,1024]{2,1,0:T(8,128)} %param.15) | copy-start | bytes 196612
  68.3 9.5 %collective-permute-start.2 = (f32[32,2,1,1024]{3,0,2,1:T(8,128)S(1)}, f32[32,2,1,1024]{3,0,2,1:T(8,128)S(1)}, u32[]{:S(2)}, u32[]{:S(2)}) collective-permute-start(f32[32,2,1,1024]{3,0,2,1:T(8,128)S(1)} %get-tuple-element.48), channel_id=1, source_target_pairs={{4,0},{8,4},{12,8},{16,12},{20,16},{24,20},{28,24},{32,28},{36,32}... | collective-permute-start | bytes 786440 | tf_op jit(solution)/shard_map/ppermute | solution.py:18
  69.7 8.1 %copy-start.7 = (f32[32,2,8,1024]{3,2,1,0:T(8,128)S(1)}, f32[32,2,8,1024]{3,2,1,0:T(8,128)}, u32[]{:S(2)}) copy-start(f32[32,2,8,1024]{3,2,1,0:T(8,128)} %param.12) | copy-start | bytes 6291460
  70.5 13.2 %copy-start.5 = (f32[32,2,8,1023]{3,0,2,1:T(8,128)}, f32[32,2,8,1023]{3,0,2,1:T(8,128)S(1)}, u32[]{:S(2)}) copy-start(f32[32,2,8,1023]{3,0,2,1:T(8,128)S(1)} %get-tuple-element.50) | copy-start | bytes 6285316
  70.5 13.2 %copy-start.6 = (f32[32,2,8,1023]{3,0,2,1:T(8,128)}, f32[32,2,8,1023]{3,0,2,1:T(8,128)S(1)}, u32[]{:S(2)}) copy-start(f32[32,2,8,1023]{3,0,2,1:T(8,128)S(1)} %get-tuple-element.51) | copy-start | bytes 6285316
  86.1 56.0 %collective-permute-start.1 = (f32[2,32,2,1,1024]{4,1,3,2,0:T(8,128)}, f32[2,32,2,1,1024]{4,1,3,2,0:T(8,128)}, u32[]{:S(2)}, u32[]{:S(2)}) collective-permute-start(f32[2,32,2,1,1024]{4,1,3,2,0:T(8,128)} %get-tuple-element.28), channel_id=1, source_target_pairs={{4,0},{8,4},{12,8},{16,12},{20,16},{24,20},{28,24},{32,28},{36,32}... | collective-permute-start | bytes 1572872 | tf_op jit(solution)/shard_map/ppermute | solution.py:18
  87.4 54.7 %collective-permute-start = (f32[2,32,2,1,1024]{4,1,3,2,0:T(8,128)}, f32[2,32,2,1,1024]{4,1,3,2,0:T(8,128)}, u32[]{:S(2)}, u32[]{:S(2)}) collective-permute-start(f32[2,32,2,1,1024]{4,1,3,2,0:T(8,128)} %get-tuple-element.27), channel_id=1, source_target_pairs={{0,4},{4,8},{8,12},{12,16},{16,20},{20,24},{24,28},{28,32},{32,36}... | collective-permute-start | bytes 1572872 | tf_op jit(solution)/shard_map/ppermute | solution.py:17
  92.8 108.9 %all-reduce.9.cloned.1.call-start = ((), (), s32[]{:S(2)}) async-start(), calls=%async_computation.5 | async-start | bytes 131072 | tf_op jit(solution)/shard_map/psum | solution.py:95
  157.0 122.7 %all-reduce.11.cloned.1.call-start = ((), (), s32[]{:S(2)}) async-start(), calls=%async_computation.6 | async-start | bytes 131072 | tf_op jit(solution)/shard_map/psum | solution.py:95
  159.0 55.9 %collective-permute-start.6 = (f32[32,2,1,1024]{3,0,2,1:T(8,128)}, f32[32,2,1,1024]{3,0,2,1:T(8,128)}, u32[]{:S(2)}, u32[]{:S(2)}) collective-permute-start(f32[32,2,1,1024]{3,0,2,1:T(8,128)} %get-tuple-element.43), channel_id=1, source_target_pairs={{4,0},{8,4},{12,8},{16,12},{20,16},{24,20},{28,24},{32,28},{36,32}... | collective-permute-start | bytes 786440 | tf_op jit(solution)/shard_map/ppermute | solution.py:18
  160.3 54.6 %collective-permute-start.7 = (f32[32,2,1,1024]{3,0,2,1:T(8,128)}, f32[32,2,1,1024]{3,0,2,1:T(8,128)}, u32[]{:S(2)}, u32[]{:S(2)}) collective-permute-start(f32[32,2,1,1024]{3,0,2,1:T(8,128)} %get-tuple-element.42), channel_id=1, source_target_pairs={{0,4},{4,8},{8,12},{12,16},{16,20},{20,24},{24,28},{28,32},{32,36}... | collective-permute-start | bytes 786440 | tf_op jit(solution)/shard_map/ppermute | solution.py:17
  208.3 6.6 %copy-start.11 = (f32[32,2,8,1023]{3,0,2,1:T(8,128)S(1)}, f32[32,2,8,1023]{3,0,2,1:T(8,128)}, u32[]{:S(2)}) copy-start(f32[32,2,8,1023]{3,0,2,1:T(8,128)} %get-tuple-element.44) | copy-start | bytes 6285316
  208.3 6.6 %copy-start.12 = (f32[32,2,8,1023]{3,0,2,1:T(8,128)S(1)}, f32[32,2,8,1023]{3,0,2,1:T(8,128)}, u32[]{:S(2)}) copy-start(f32[32,2,8,1023]{3,0,2,1:T(8,128)} %get-tuple-element.45) | copy-start | bytes 6285316
  209.0 15.8 %collective-permute-start.5 = (f32[2,32,2,1,1024]{4,1,3,2,0:T(8,128)S(1)}, f32[2,32,2,1,1024]{4,1,3,2,0:T(8,128)S(1)}, u32[]{:S(2)}, u32[]{:S(2)}) collective-permute-start(f32[2,32,2,1,1024]{4,1,3,2,0:T(8,128)S(1)} %get-tuple-element.26), channel_id=1, source_target_pairs={{4,0},{8,4},{12,8},{16,12},{20,16},{24,20},{28,24},{32,28},{36,32}... | collective-permute-start | bytes 1572872 | tf_op jit(solution)/shard_map/ppermute | solution.py:18
  210.5 15.1 %collective-permute-start.4 = (f32[2,32,2,1,1024]{4,1,3,2,0:T(8,128)S(1)}, f32[2,32,2,1,1024]{4,1,3,2,0:T(8,128)S(1)}, u32[]{:S(2)}, u32[]{:S(2)}) collective-permute-start(f32[2,32,2,1,1024]{4,1,3,2,0:T(8,128)S(1)} %get-tuple-element.25), channel_id=1, source_target_pairs={{0,4},{4,8},{8,12},{12,16},{16,20},{20,24},{24,28},{28,32},{32,36}... | collective-permute-start | bytes 1572872 | tf_op jit(solution)/shard_map/ppermute | solution.py:17
  228.1 51.6 %copy-start.33 = (f32[32]{0:T(128)S(1)}, f32[32]{0:T(128)}, u32[]{:S(2)}) copy-start(f32[32]{0:T(128)} %get-tuple-element.56) | copy-start | bytes 388
  231.7 81.1 %reduce-scatter.4.cloned.1.call-start = ((), (), s32[]{:S(2)}) async-start(), calls=%async_computation.7 | async-start | bytes 81920 | tf_op jit(solution)/shard_map/reduce_scatter | solution.py:75
  232.4 114.6 %reduce-scatter.6.cloned.1.call-start = ((), (), s32[]{:S(2)}) async-start(), calls=%async_computation.8 | async-start | bytes 81920 | tf_op jit(solution)/shard_map/reduce_scatter | solution.py:76
  233.2 148.2 %reduce-scatter.8.cloned.1.call-start = ((), (), s32[]{:S(2)}) async-start(), calls=%async_computation.9 | async-start | bytes 81920 | tf_op jit(solution)/shard_map/reduce_scatter | solution.py:77
  (25 other events, 96.1 us)
Sparse Core Ops, SparseCore 0:
  11.8 49.3 all-reduce.4
  93.0 48.2 all-reduce.6
  157.2 44.5 all-reduce.8
  231.8 47.8 all-reduce.10
  282.8 29.9 reduce-scatter.3
  316.0 31.0 reduce-scatter.5
  350.3 31.0 reduce-scatter.7
where the time goes:
time: 389 us; the launch traced here: 388 us
  waiting for transfers between devices  285 us (73%)
  other arithmetic  43 us (11%)
  starting transfers between devices  22.7 us (6%)
  local copies, waits for them, and re-layouts  22.4 us (6%)
  between operations  14.7 us (4%)
    psum x2, waiting for transfers between devices, local(): crowd = lax.psum(jnp.sum(weight * state, axis=0), 'coh') / COH  91 us
    psum x2, waiting for transfers between devices, local(): lax.psum(jnp.sum(-crowding * grad_surv * survived, axis=0), 'coh')  82.6 us
    reduce_scatter x1, waiting for transfers between devices, local(): lax.psum_scatter(grad_kappa, 'coh', scatter_dimension=2, tiled=True)  34.3 us
    reduce_scatter x1, waiting for transfers between devices, local(): lax.psum_scatter(grad_north, 'coh', scatter_dimension=2, tiled=True)  34.2 us
    reduce_scatter x1, waiting for transfers between devices, local(): lax.psum_scatter(grad_east, 'coh', scatter_dimension=2, tiled=True)  29.2 us
    ppermute x4, starting transfers between devices, extended(): before = lax.ppermute(last, axis, up)  16.8 us
    reduce_sum x2, other arithmetic, local(): grad_kappa = jnp.sum(masked * laplace, axis=0)  9.98 us
    ppermute x4, waiting for transfers between devices, extended(): after = lax.ppermute(first, axis, down)  9.14 us
  transfers between devices with their start and end apart: 15, of which 11 were waited for; matrix products, arithmetic and copies ran while one was open for 7% of the time, Pallas kernels for 0%

commit v1 on v0

--- a/solution.py
+++ b/solution.py
@@ -49,7 +49,7 @@
     state = density
     saved = []
     for section in range(STEPS):
-        crowd = lax.psum(jnp.sum(weight * state, axis=0), "coh") / COH
+        crowd = jnp.sum(lax.all_gather(jnp.sum(weight * state, axis=0), "coh"), axis=0) / COH
         survival = jnp.exp(-(mortal + crowding * crowd[None]))
         survived = state * survival
         wet = ocean * survived

time: 389 us -> 322 us (0.83)
  waiting for transfers between devices: 285 us -> 203 us
  blocking collectives: 0 us -> 19.4 us
    psum x2 -> x0, waiting for transfers between devices: 91 us -> none  [local(): crowd = lax.psum(jnp.sum(weight * state, axis=0), 'coh') / COH]
    all_gather x0 -> x2, blocking collectives: none -> 19.4 us  [local(): lax.all_gather(jnp.sum(weight * state, axis=0), 'coh')]
    psum x2, waiting for transfers between devices: 82.6 us -> 92.5 us  [local(): lax.psum(jnp.sum(-crowding * grad_surv * survived, axis=0), 'coh')]
  transfers between devices with their start and end apart: 15 -> 13, of which waited for: 11 -> 9; matrix products, arithmetic and copies ran while one was open for 7% -> 8% of each run, Pallas kernels for 0% -> 0%
where the time goes in v1:
time: 322 us; the launch traced here: 321 us
  waiting for transfers between devices  203 us (63%)
  other arithmetic  42.2 us (13%)
  starting transfers between devices  22.1 us (7%)
  blocking collectives  19.4 us (6%)
  local copies, waits for them, and re-layouts  19.1 us (6%)
  between operations  14.3 us (4%)
    psum x2, waiting for transfers between devices, local(): lax.psum(jnp.sum(-crowding * grad_surv * survived, axis=0), 'coh')  92.5 us
    reduce_scatter x1, waiting for transfers between devices, local(): lax.psum_scatter(grad_north, 'coh', scatter_dimension=2, tiled=True)  34.2 us
    reduce_scatter x1, waiting for transfers between devices, local(): lax.psum_scatter(grad_kappa, 'coh', scatter_dimension=2, tiled=True)  34.2 us
    reduce_scatter x1, waiting for transfers between devices, local(): lax.psum_scatter(grad_east, 'coh', scatter_dimension=2, tiled=True)  29.3 us
    all_gather x2, blocking collectives, local(): lax.all_gather(jnp.sum(weight * state, axis=0), 'coh')  19.4 us
    ppermute x4, starting transfers between devices, extended(): before = lax.ppermute(last, axis, up)  16.4 us
    reduce_sum x2, other arithmetic, local(): grad_kappa = jnp.sum(masked * laplace, axis=0)  9.92 us
    ppermute x4, waiting for transfers between devices, extended(): after = lax.ppermute(first, axis, down)  9.5 us
  transfers between devices with their start and end apart: 13, of which 9 were waited for; matrix products, arithmetic and copies ran while one was open for 8% of the time, Pallas kernels for 0%

profile of v1, /device:TPU:1, one launch (start us, length us, event | category | flops | bytes accessed | tf_op | source)
XLA Modules:
  0.0 321.1 jit_solution(662250210040617315)
XLA Ops:
  8.1 2.8 multiply_reduce_fusion.9
  11.0 10.3 %all-gather = f32[8,8,1024]{2,1,0:T(8,128)S(1)} all-gather(f32[2,8,1024]{2,1,0:T(8,128)S(1)} %multiply_reduce_fusion.9), channel_id=2, replica_groups=mesh['lat'=64,'coh'=4] {'coh'}, dimensions={0}, use_global_device_ids=true | all-gather | bytes 327680 | tf_op jit(solution)/shard_map/all_gather | solution.py:52
  21.4 3.0 fusion.26
  24.4 2.0 collective-permute-start.3
  29.5 2.4 collective-permute-done.3
  31.9 4.4 %collective-permute-done.2 = f32[32,2,1,1024]{3,0,2,1:T(8,128)S(1)} collective-permute-done((f32[32,2,1,1024]{3,0,2,1:T(8,128)S(1)}, f32[32,2,1,1024]{3,0,2,1:T(8,128)S(1)}, u32[]{:S(2)}, u32[]{:S(2)}) %collective-permute-start.2) | collective-permute-done | bytes 262176 | tf_op jit(solution)/shard_map/ppermute | solution.py:18
  36.2 5.0 %fusion.9 = (f32[32,2,8,1024]{3,0,2,1:T(8,128)}, f32[32,2,8,1024]{3,0,2,1:T(8,128)S(1)}, f32[1,32,2,8,1024]{4,1,3,2,0:T(8,128)S(1)}, f32[1,32,2,8,1024]{4,1,3,2,...) fusion(f32[2,8,1024]{2,1,0:T(8,128)S(1)} %copy-done.21, f32[32]{0:T(128)S(1)} %get-tuple-element.58, ...), kind=kLoop, calls=%fused_computation.15 | loop fusion | flops 18333696 | bytes 19726592 | tf_op jit(solution)/shard_map/mul | solution.py:82
  44.9 5.0 %collective-permute-start = (f32[2,32,2,1,1024]{4,1,3,2,0:T(8,128)}, f32[2,32,2,1,1024]{4,1,3,2,0:T(8,128)}, u32[]{:S(2)}, u32[]{:S(2)}) collective-permute-start(f32[2,32,2,1,1024]{4,1,3,2,0:T(8,128)} %get-tuple-element.27), channel_id=1, source_target_pairs={{0,4},{4,8},{8,12},{12,16},{16,20},{20,24},{24,28},{28,32},{32,36}... | collective-permute-start | bytes 1572872 | tf_op jit(solution)/shard_map/ppermute | solution.py:17
  52.4 9.0 %all-gather.1 = f32[8,8,1024]{2,1,0:T(8,128)} all-gather(f32[2,8,1024]{2,1,0:T(8,128)S(1)} %get-tuple-element.54), channel_id=3, replica_groups=mesh['lat'=64,'coh'=4] {'coh'}, dimensions={0}, use_global_device_ids=true | all-gather | bytes 327680 | tf_op jit(solution)/shard_map/all_gather | solution.py:52
  65.0 3.1 pad_maximum_fusion
  71.6 4.5 %multiply_reduce_fusion.7 = (f32[2,8,1024]{2,1,0:T(8,128)}, f32[32,2,8,1024]{3,0,2,1:T(8,128)}, f32[32,2,8,1024]{3,0,2,1:T(8,128)S(1)}) fusion(f32[32,2,8,1024]{3,0,2,1:T(8,128)S(1)} %copy-done.13, f32[32]{0:T(128)S(1)} %get-tuple-element.57, f32[2,8,1024]{2,1,0:T(8,128)S(1)} %broadcast_multiply_fusion, f32[32]{0:T(128)S(1)} %get-tuple-element.60, ...), kind=kLoop, calls=%fused_computation.57 | loop fusion | flops 8896512 | bytes 17039744 | tf_op jit(solution)/shard_map/reduce_sum | solution.py:95
  76.1 2.9 fusion.42
  83.0 5.2 %collective-permute-start.7 = (f32[32,2,1,1024]{3,0,2,1:T(8,128)}, f32[32,2,1,1024]{3,0,2,1:T(8,128)}, u32[]{:S(2)}, u32[]{:S(2)}) collective-permute-start(f32[32,2,1,1024]{3,0,2,1:T(8,128)} %get-tuple-element.42), channel_id=1, source_target_pairs={{0,4},{4,8},{8,12},{12,16},{16,20},{20,24},{24,28},{28,32},{32,36}... | collective-permute-start | bytes 786440 | tf_op jit(solution)/shard_map/ppermute | solution.py:17
  88.3 46.6 %all-reduce.3.cloned.1.call-done = f32[2,8,1024]{2,1,0:T(8,128)} async-done(((f32[2,8,1024]{2,1,0:T(8,128)}), f32[2,8,1024]{2,1,0:T(8,128)}) %all-reduce.3.cloned.1.call-update) | async-done | bytes 65552 | tf_op jit(solution)/shard_map/psum | solution.py:95
  134.9 5.2 %multiply_reduce_fusion = (f32[2,8,1024]{2,1,0:T(8,128)}, f32[2,8,1024]{2,1,0:T(8,128)}, f32[2,8,1024]{2,1,0:T(8,128)}, f32[32,2,8,1024]{3,0,2,1:T(8,128)S(1)}) fusion(f32[32,2,8,1024]{3,0,2,1:T(8,128)S(1)} %fusion.26, f32[32,2,8,1023]{3,0,2,1:T(8,128)} %copy-done.6, f32[32,2,8,1]{3,0,2,1:T(8,128)S(1)} %get-tuple-element.53, ...), kind=kLoop, calls=%fused_computation.48 | loop fusion | flops 14106624 | bytes 11403776 | tf_op jit(solution)/shard_map/reduce_sum | solution.py:73
  143.7 4.2 %collective-permute-start.4 = (f32[2,32,2,1,1024]{4,1,3,2,0:T(8,128)S(1)}, f32[2,32,2,1,1024]{4,1,3,2,0:T(8,128)S(1)}, u32[]{:S(2)}, u32[]{:S(2)}) collective-permute-start(f32[2,32,2,1,1024]{4,1,3,2,0:T(8,128)S(1)} %get-tuple-element.25), channel_id=1, source_target_pairs={{0,4},{4,8},{8,12},{12,16},{16,20},{20,24},{24,28},{28,32},{32,36}... | collective-permute-start | bytes 1572872 | tf_op jit(solution)/shard_map/ppermute | solution.py:17
  148.1 4.7 %multiply_reduce_fusion.1 = (f32[2,8,1024]{2,1,0:T(8,128)}, f32[2,8,1024]{2,1,0:T(8,128)}, f32[2,8,1024]{2,1,0:T(8,128)}) fusion(f32[32,2,8,1024]{3,0,2,1:T(8,128)S(1)} %copy-done.1, f32[32,2,8,1023]{3,0,2,1:T(8,128)S(1)} %copy-done.12, f32[32,2,8,1]{3,0,2,1:T(8,128)S(1)} %copy-done.15, f32[32,2,8,1]{3,0,2,1:T(8,128)S(1)} %get-tuple-element.46, ...), kind=kLoop, calls=%fused_computation.49 | loop fusion | flops 10960896 | bytes 9175168 | tf_op jit(solution)/shard_map/reduce_sum | solution.py:73
  152.8 5.1 %collective-permute-done.5 = f32[2,32,2,1,1024]{4,1,3,2,0:T(8,128)S(1)} collective-permute-done((f32[2,32,2,1,1024]{4,1,3,2,0:T(8,128)S(1)}, f32[2,32,2,1,1024]{4,1,3,2,0:T(8,128)S(1)}, u32[]{:S(2)}, u32[]{:S(2)}) %collective-permute-start.5) | collective-permute-done | bytes 524320 | tf_op jit(solution)/shard_map/ppermute | solution.py:18
  161.3 3.6 %multiply_reduce_fusion.6 = (f32[2,8,1024]{2,1,0:T(8,128)}, f32[32,2,8,1024]{3,0,2,1:T(8,128)S(1)}) fusion(f32[32,2,8,1024]{3,2,1,0:T(8,128)S(1)} %copy-done.2, f32[32]{0:T(128)S(1)} %get-tuple-element.57, f32[2,8,1024]{2,1,0:T(8,128)S(1)} %broadcast_multiply_fusion.1, f32[32]{0:T(128)S(1)} %get-tuple-element.60, f32[32]{0:T(128)S(1)} %get-tuple-element.61, ...), kind=kLoop, calls=%fused_computation.55 | loop fusion | flops 7847936 | bytes 14942592 | tf_op jit(solution)/shard_map/reduce_sum | solution.py:95
  167.0 45.8 %all-reduce.5.cloned.1.call-done = f32[2,8,1024]{2,1,0:T(8,128)} async-done(((f32[2,8,1024]{2,1,0:T(8,128)}), f32[2,8,1024]{2,1,0:T(8,128)}) %all-reduce.5.cloned.1.call-update) | async-done | bytes 65552 | tf_op jit(solution)/shard_map/psum | solution.py:95
  214.3 2.5 copy.18
  216.8 29.3 %reduce-scatter.4.cloned.1.call-done = f32[2,8,256]{2,1,0:T(8,128)} async-done(((f32[2,8,1024]{2,1,0:T(8,128)}), f32[2,8,256]{2,1,0:T(8,128)}) %reduce-scatter.4.cloned.1.call-update) | async-done | bytes 16400 | tf_op jit(solution)/shard_map/reduce_scatter | solution.py:75
  246.2 34.2 %reduce-scatter.6.cloned.1.call-done = f32[2,8,256]{2,1,0:T(8,128)} async-done(((f32[2,8,1024]{2,1,0:T(8,128)}), f32[2,8,256]{2,1,0:T(8,128)}) %reduce-scatter.6.cloned.1.call-update) | async-done | bytes 16400 | tf_op jit(solution)/shard_map/reduce_scatter | solution.py:76
  280.4 34.2 %reduce-scatter.8.cloned.1.call-done = f32[2,8,256]{2,1,0:T(8,128)} async-done(((f32[2,8,1024]{2,1,0:T(8,128)}), f32[2,8,256]{2,1,0:T(8,128)}) %reduce-scatter.8.cloned.1.call-update) | async-done | bytes 16400 | tf_op jit(solution)/shard_map/reduce_scatter | solution.py:77
  (115 shorter events, 31.6 us)
Async XLA Ops:
  7.2 14.2 %copy-start.31 = (s32[2,8,1024]{2,1,0:T(8,128)S(1)}, s32[2,8,1024]{2,1,0:T(8,128)}, u32[]{:S(2)}) copy-start(s32[2,8,1024]{2,1,0:T(8,128)} %param.13) | copy-start | bytes 196612
  7.2 127.7 %all-reduce.3.cloned.1.call-start = ((), (), s32[]{:S(2)}) async-start(), calls=%async_computation.3 | async-start | bytes 131072 | tf_op jit(solution)/shard_map/psum | solution.py:95
  24.4 7.5 %collective-permute-start.3 = (f32[32,2,1,1024]{3,0,2,1:T(8,128)S(1)}, f32[32,2,1,1024]{3,0,2,1:T(8,128)S(1)}, u32[]{:S(2)}, u32[]{:S(2)}) collective-permute-start(f32[32,2,1,1024]{3,0,2,1:T(8,128)S(1)} %get-tuple-element.49), channel_id=1, source_target_pairs={{0,4},{4,8},{8,12},{12,16},{16,20},{20,24},{24,28},{28,32},{32,36}... | collective-permute-start | bytes 786440 | tf_op jit(solution)/shard_map/ppermute | solution.py:17
  26.4 9.8 %copy-start.21 = (f32[2,8,1024]{2,1,0:T(8,128)S(1)}, f32[2,8,1024]{2,1,0:T(8,128)}, u32[]{:S(2)}) copy-start(f32[2,8,1024]{2,1,0:T(8,128)} %param.14) | copy-start | bytes 196612
  26.4 9.8 %copy-start.23 = (f32[2,8,1024]{2,1,0:T(8,128)S(1)}, f32[2,8,1024]{2,1,0:T(8,128)}, u32[]{:S(2)}) copy-start(f32[2,8,1024]{2,1,0:T(8,128)} %param.15) | copy-start | bytes 196612
  26.4 9.8 %collective-permute-start.2 = (f32[32,2,1,1024]{3,0,2,1:T(8,128)S(1)}, f32[32,2,1,1024]{3,0,2,1:T(8,128)S(1)}, u32[]{:S(2)}, u32[]{:S(2)}) collective-permute-start(f32[32,2,1,1024]{3,0,2,1:T(8,128)S(1)} %get-tuple-element.48), channel_id=1, source_target_pairs={{4,0},{8,4},{12,8},{16,12},{20,16},{24,20},{28,24},{32,28},{36,32}... | collective-permute-start | bytes 786440 | tf_op jit(solution)/shard_map/ppermute | solution.py:18
  27.9 8.4 %copy-start.7 = (f32[32,2,8,1024]{3,2,1,0:T(8,128)S(1)}, f32[32,2,8,1024]{3,2,1,0:T(8,128)}, u32[]{:S(2)}) copy-start(f32[32,2,8,1024]{3,2,1,0:T(8,128)} %param.12) | copy-start | bytes 6291460
  28.6 12.6 %copy-start.5 = (f32[32,2,8,1023]{3,0,2,1:T(8,128)}, f32[32,2,8,1023]{3,0,2,1:T(8,128)S(1)}, u32[]{:S(2)}) copy-start(f32[32,2,8,1023]{3,0,2,1:T(8,128)S(1)} %get-tuple-element.50) | copy-start | bytes 6285316
  28.7 12.6 %copy-start.6 = (f32[32,2,8,1023]{3,0,2,1:T(8,128)}, f32[32,2,8,1023]{3,0,2,1:T(8,128)S(1)}, u32[]{:S(2)}) copy-start(f32[32,2,8,1023]{3,0,2,1:T(8,128)S(1)} %get-tuple-element.51) | copy-start | bytes 6285316
  43.6 21.3 %collective-permute-start.1 = (f32[2,32,2,1,1024]{4,1,3,2,0:T(8,128)}, f32[2,32,2,1,1024]{4,1,3,2,0:T(8,128)}, u32[]{:S(2)}, u32[]{:S(2)}) collective-permute-start(f32[2,32,2,1,1024]{4,1,3,2,0:T(8,128)} %get-tuple-element.28), channel_id=1, source_target_pairs={{4,0},{8,4},{12,8},{16,12},{20,16},{24,20},{28,24},{32,28},{36,32}... | collective-permute-start | bytes 1572872 | tf_op jit(solution)/shard_map/ppermute | solution.py:18
  44.9 20.1 %collective-permute-start = (f32[2,32,2,1,1024]{4,1,3,2,0:T(8,128)}, f32[2,32,2,1,1024]{4,1,3,2,0:T(8,128)}, u32[]{:S(2)}, u32[]{:S(2)}) collective-permute-start(f32[2,32,2,1,1024]{4,1,3,2,0:T(8,128)} %get-tuple-element.27), channel_id=1, source_target_pairs={{0,4},{4,8},{8,12},{12,16},{16,20},{20,24},{24,28},{28,32},{32,36}... | collective-permute-start | bytes 1572872 | tf_op jit(solution)/shard_map/ppermute | solution.py:17
  79.8 133.1 %all-reduce.5.cloned.1.call-start = ((), (), s32[]{:S(2)}) async-start(), calls=%async_computation.4 | async-start | bytes 131072 | tf_op jit(solution)/shard_map/psum | solution.py:95
  81.7 66.3 %collective-permute-start.6 = (f32[32,2,1,1024]{3,0,2,1:T(8,128)}, f32[32,2,1,1024]{3,0,2,1:T(8,128)}, u32[]{:S(2)}, u32[]{:S(2)}) collective-permute-start(f32[32,2,1,1024]{3,0,2,1:T(8,128)} %get-tuple-element.43), channel_id=1, source_target_pairs={{4,0},{8,4},{12,8},{16,12},{20,16},{24,20},{28,24},{32,28},{36,32}... | collective-permute-start | bytes 786440 | tf_op jit(solution)/shard_map/ppermute | solution.py:18
  83.0 65.0 %collective-permute-start.7 = (f32[32,2,1,1024]{3,0,2,1:T(8,128)}, f32[32,2,1,1024]{3,0,2,1:T(8,128)}, u32[]{:S(2)}, u32[]{:S(2)}) collective-permute-start(f32[32,2,1,1024]{3,0,2,1:T(8,128)} %get-tuple-element.42), channel_id=1, source_target_pairs={{0,4},{4,8},{8,12},{12,16},{16,20},{20,24},{24,28},{28,32},{32,36}... | collective-permute-start | bytes 786440 | tf_op jit(solution)/shard_map/ppermute | solution.py:17
  141.4 6.6 %copy-start.11 = (f32[32,2,8,1023]{3,0,2,1:T(8,128)S(1)}, f32[32,2,8,1023]{3,0,2,1:T(8,128)}, u32[]{:S(2)}) copy-start(f32[32,2,8,1023]{3,0,2,1:T(8,128)} %get-tuple-element.44) | copy-start | bytes 6285316
  141.4 6.6 %copy-start.12 = (f32[32,2,8,1023]{3,0,2,1:T(8,128)S(1)}, f32[32,2,8,1023]{3,0,2,1:T(8,128)}, u32[]{:S(2)}) copy-start(f32[32,2,8,1023]{3,0,2,1:T(8,128)} %get-tuple-element.45) | copy-start | bytes 6285316
  142.0 6.0 %copy-start.1 = (f32[32,2,8,1024]{3,0,2,1:T(8,128)S(1)}, f32[32,2,8,1024]{3,0,2,1:T(8,128)}, u32[]{:S(2)}) copy-start(f32[32,2,8,1024]{3,0,2,1:T(8,128)} %copy-done) | copy-start | bytes 6291460
  142.0 6.0 %copy-start.9 = (f32[32,2,8,1024]{3,2,1,0:T(8,128)S(1)}, f32[32,2,8,1024]{3,2,1,0:T(8,128)}, u32[]{:S(2)}) copy-start(f32[32,2,8,1024]{3,2,1,0:T(8,128)} %param.12) | copy-start | bytes 6291460
  142.1 15.8 %collective-permute-start.5 = (f32[2,32,2,1,1024]{4,1,3,2,0:T(8,128)S(1)}, f32[2,32,2,1,1024]{4,1,3,2,0:T(8,128)S(1)}, u32[]{:S(2)}, u32[]{:S(2)}) collective-permute-start(f32[2,32,2,1,1024]{4,1,3,2,0:T(8,128)S(1)} %get-tuple-element.26), channel_id=1, source_target_pairs={{4,0},{8,4},{12,8},{16,12},{20,16},{24,20},{28,24},{32,28},{36,32}... | collective-permute-start | bytes 1572872 | tf_op jit(solution)/shard_map/ppermute | solution.py:18
  143.7 15.1 %collective-permute-start.4 = (f32[2,32,2,1,1024]{4,1,3,2,0:T(8,128)S(1)}, f32[2,32,2,1,1024]{4,1,3,2,0:T(8,128)S(1)}, u32[]{:S(2)}, u32[]{:S(2)}) collective-permute-start(f32[2,32,2,1,1024]{4,1,3,2,0:T(8,128)S(1)} %get-tuple-element.25), channel_id=1, source_target_pairs={{0,4},{4,8},{8,12},{12,16},{16,20},{20,24},{24,28},{28,32},{32,36}... | collective-permute-start | bytes 1572872 | tf_op jit(solution)/shard_map/ppermute | solution.py:17
  161.3 51.6 %copy-start.32 = (f32[32]{0:T(128)S(1)}, f32[32]{0:T(128)}, u32[]{:S(2)}) copy-start(f32[32]{0:T(128)} %get-tuple-element.56) | copy-start | bytes 388
  164.9 81.3 %reduce-scatter.4.cloned.1.call-start = ((), (), s32[]{:S(2)}) async-start(), calls=%async_computation.5 | async-start | bytes 81920 | tf_op jit(solution)/shard_map/reduce_scatter | solution.py:75
  165.6 114.7 %reduce-scatter.6.cloned.1.call-start = ((), (), s32[]{:S(2)}) async-start(), calls=%async_computation.6 | async-start | bytes 81920 | tf_op jit(solution)/shard_map/reduce_scatter | solution.py:76
  166.3 148.2 %reduce-scatter.8.cloned.1.call-start = ((), (), s32[]{:S(2)}) async-start(), calls=%async_computation.7 | async-start | bytes 81920 | tf_op jit(solution)/shard_map/reduce_scatter | solution.py:77
  (22 other events, 78.2 us)
Sparse Core Ops, SparseCore 0:
  79.9 54.9 all-reduce.2
  165.0 47.8 all-reduce.4
  216.1 29.9 reduce-scatter.3
  249.3 31.0 reduce-scatter.5
  283.4 31.0 reduce-scatter.7
